TPU v7x, 32 devices: a whole 2x2x4 slice. The times are simulated.
32 devices in a mesh: item: 8 (over z, y), code: 4 (over x, core).
Axes of the slice: x: 2, y: 2, z: 4, core: 2. Of those that a mesh axis runs over, the one named last changes fastest.
Arguments:
- residuals: float32 [256, 32768], P('code', 'item'), may hold values from -6 to 6
- codebook: float32 [256, 32768], P('item', 'code'), may hold values from -6 to 6
- item_weight: float32 [32768], P('item'), may hold values from 1 to 100
- code_capacity: float32 [32768], P('code'), may hold values from 0.25 to 4
- pairs: int32 [512, 64], P('item', 'code'), may hold values from -1 to 127, as said below
Outputs:
- item_potential: float32 [32768], P('item')
- code_potential: float32 [32768], P('code')
Inputs may be any that keep to these rules, and one draw needn't show every extreme that they name: `pairs`: each entry is -1 (no candidate) or a code block's number within the code shard of its slot column. Within one item block and one code shard the live entries are distinct, the first slot is always live, and between 1 and 8 are live; some device holds exactly 8 live slots in every item block. Every code block is named by some item block.
All inputs are finite; a program needn't handle non-finite values.
Results may differ from a plain program's by a relative error of at most 0.0003.
Values sent between devices are 32-bit elements; how exact they have to be, the bound alone decides.
No kernel may reach another device: no remote copies, remote signals or barrier semaphores. Data moves between devices by JAX's collectives and lax.ppermute only.
A program may use at most 128 MiB of HBM per device.

v0:
```python
import math
import jax
import jax.numpy as jnp
from jax import lax
from jax.sharding import PartitionSpec as P

BLOCK = 64
ITERS = 3
masked_score = -1e30
softness_factor = 0.1


def body(residuals, codebook, item_weight, code_capacity, pairs):
    item_columns = lax.all_gather(residuals, "code", axis=0, tiled=True)
    code_cols = lax.all_gather(codebook, "item", axis=0, tiled=True)
    embedding_width = item_columns.shape[0]
    item_count = item_columns.shape[1]
    code_count = code_cols.shape[1]
    item_blocks = item_count // BLOCK
    code_blocks = code_count // BLOCK
    logit_scale = 1.0 / (softness_factor * math.sqrt(embedding_width))
    weight_sum = lax.psum(jnp.sum(item_weight), "item")
    capacity_sum = lax.psum(jnp.sum(code_capacity), "code")
    item_logmass = jnp.log(item_weight) - jnp.log(weight_sum)
    code_logmass = jnp.log(code_capacity) - jnp.log(capacity_sum)
    slot_order = jnp.argsort((pairs < 0).astype(jnp.int32), axis=1, stable=True)[
        :, : pairs.shape[1] // 2
    ]
    chosen = jnp.take_along_axis(pairs, slot_order, axis=1)
    is_live = chosen >= 0
    safe_ids = jnp.where(is_live, chosen, 0)
    target = jnp.where(is_live, chosen, code_blocks)
    item_split_cols = item_columns.reshape(embedding_width, item_blocks, BLOCK)
    code_column_splits = code_cols.reshape(embedding_width, code_blocks, BLOCK)
    group = math.gcd(item_blocks, 8)
    group_count = item_blocks // group

    def build_tiles(own, ids, live):
        picked = code_column_splits[:, ids, :]
        scores = (
            jnp.einsum("rbi,rbsj->bsij", own, picked, precision=lax.Precision.HIGHEST) * logit_scale
        )
        return jnp.where(live[:, :, None, None], scores, masked_score)

    reduce_fn = lambda tiles, ids, portion: tiles

    def one_group(group_index):
        start = group_index * group
        own = lax.dynamic_slice_in_dim(item_split_cols, start, group, 1)
        ids = lax.dynamic_slice_in_dim(safe_ids, start, group, 0)
        live = lax.dynamic_slice_in_dim(is_live, start, group, 0)
        portion = lax.dynamic_slice_in_dim(safe_ids, start, group, 0)
        return reduce_fn(build_tiles(own, ids, live), ids, portion)

    results = lax.map(one_group, jnp.arange(group_count, dtype=jnp.int32))
    saved_tile_blocks = results.reshape((item_blocks,) + results.shape[2:])

    def run_pass(reduce_fn, extra):
        return reduce_fn(saved_tile_blocks, safe_ids, extra)

    flat_target = target.reshape(-1)
    flat_rows = flat_target.shape[0]
    row_group = math.gcd(flat_rows, 256)
    one_hot = flat_target[:, None] == jnp.arange(code_blocks, dtype=jnp.int32)[None, :]
    one_hot_groups = one_hot.reshape(flat_rows // row_group, row_group, code_blocks)
    one_hot_float = one_hot.astype(jnp.float32)
    code_potential = jnp.zeros((code_count,), jnp.float32)
    item_potential = jnp.zeros((item_count,), jnp.float32)
    for sweep in range(ITERS):
        code_split = code_potential.reshape(code_blocks, BLOCK)

        def row_reduce(tiles, ids, portion):
            logits = tiles + code_split[ids][:, :, None, :]
            block_peak = jnp.max(logits, axis=(1, 3))
            block_total = jnp.sum(jnp.exp(logits - block_peak[:, None, :, None]), axis=(1, 3))
            return (block_peak, block_total)

        row_peak, row_total = run_pass(row_reduce, safe_ids)
        row_peak = row_peak.reshape(item_count)
        row_total = row_total.reshape(item_count)
        merged_peak = lax.pmax(row_peak, "code")
        merged_total = lax.psum(row_total * jnp.exp(row_peak - merged_peak), "code")
        item_potential = item_logmass - (merged_peak + jnp.log(merged_total))
        item_split = item_potential.reshape(item_blocks, BLOCK)

        def col_reduce(tiles, ids, portion):
            logits = tiles + portion[:, None, :, None]
            block_peak = jnp.max(logits, axis=2)
            block_total = jnp.sum(jnp.exp(logits - block_peak[:, :, None, :]), axis=2)
            return (block_peak, block_total)

        tile_peak, tile_total = run_pass(col_reduce, item_split)
        peak_flat = tile_peak.reshape(flat_rows, BLOCK)
        total_flat = tile_total.reshape(flat_rows, BLOCK)
        peak_groups = peak_flat.reshape(flat_rows // row_group, row_group, BLOCK)

        def peak_step(carry, pieces):
            hot, peaks = pieces
            candidate = jnp.max(jnp.where(hot[:, :, None], peaks[:, None, :], masked_score), axis=0)
            return (jnp.maximum(carry, candidate), None)

        col_peak, unused = lax.scan(
            peak_step,
            jnp.full((code_blocks, BLOCK), masked_score, jnp.float32),
            (one_hot_groups, peak_groups),
        )
        padded_peak = jnp.concatenate(
            [col_peak, jnp.full((1, BLOCK), masked_score, jnp.float32)], axis=0
        )
        spread = total_flat * jnp.exp(peak_flat - padded_peak[flat_target])
        col_total = jnp.dot(
            one_hot_float.T,
            spread,
            precision=lax.Precision.HIGHEST,
            preferred_element_type=jnp.float32,
        )
        col_peak = col_peak.reshape(code_count)
        col_total = col_total.reshape(code_count)
        joined_peak = lax.pmax(col_peak, "item")
        joined_total = lax.psum(col_total * jnp.exp(col_peak - joined_peak), "item")
        code_potential = code_logmass - (joined_peak + jnp.log(joined_total))
    return (item_potential, code_potential)


def solution(mesh):
    placed = (P("code", "item"), P("item", "code"), P("item"), P("code"), P("item", "code"))
    return jax.shard_map(
        body, mesh=mesh, in_specs=placed, out_specs=(P("item"), P("code")), check_vma=False
    )
```

profile of v0, /device:TPU:0, one launch (start us, length us, event | category | flops | bytes accessed | tf_op | source)
XLA Modules:
  0.0 706.6 jit_solution(5821192888771860012)
XLA Ops:
  10.0 23.8 %psum.56 = f32[]{:T(128)} all-reduce(f32[]{:T(128)} %reduce_sum.72), channel_id=1, replica_groups=mesh['item'=8,'code'=4] {'item'}, use_global_device_ids=true, to_apply=%region_1.0 | all-reduce | flops 1 | bytes 8 | tf_op jit(solution)/shard_map/psum | solution.py:22
  52.4 121.0 %all-gather.3.cloned.1.call-done = f32[256,8192]{1,0:T(8,128)} async-done(((f32[32,8192]{1,0:T(8,128)}), f32[256,8192]{1,0:T(8,128)}) %all-gather.3.cloned.1.call-update) | async-done | bytes 8388624 | tf_op jit(solution)/shard_map/all_gather | solution.py:15
  173.4 9.0 %copy.37 = f32[256,8192]{0,1:T(8,128)} copy(f32[256,8192]{1,0:T(8,128)} %all-gather.3.cloned.1.call-done) | data formatting | bytes 16777216 | tf_op jit(solution)/shard_map/all_gather | solution.py:15
  182.4 120.6 %while.43 = (s32[]{:T(128)}, f32[8,8,8,64,64]{3,4,2,1,0:T(8,128)}, s32[8]{0:T(128)S(1)}, pred[64,8]{0,1:T(8,128)(4,1)S(1)}, s32[64,8]{0,1:T(8,128)S(1)}, /*index...) while((s32[]{:T(128)}, f32[8,8,8,64,64]{3,4,2,1,0:T(8,128)}, ...), condition=%wide.region_4.0_spmd, body=%wide.region_3.0_spmd.sunk | while | flops 805831872 | bytes 15212019 | solution.py:55
  302.9 9.4 %add_reduce_fusion.5 = f32[8,8,64]{2,1,0:T(8,128)S(1)} fusion(f32[8,8,8,64,64]{3,4,2,1,0:T(8,128)} %get-tuple-element.107, f32[8,8,8,64]{3,2,1,0:T(8,128)S(1)} %bitcast.97), kind=kLoop, calls=%fused_computation.39 | loop fusion | flops 4190208 | bytes 8536064 | tf_op jit(solution)/shard_map/reduce_max | solution.py:74
  319.0 10.2 %pmax.42 = f32[4096]{0:T(1024)S(1)} all-reduce(f32[4096]{0:T(1024)S(1)} %reshape.247), channel_id=1, replica_groups=mesh['item'=8,'code'=4] {'code'}, use_global_device_ids=true, to_apply=%region_8.9 | all-reduce | flops 4096 | bytes 32768 | tf_op jit(solution)/shard_map/pmax | solution.py:81
  329.2 11.4 %all-reduce.3 = (f32[4096]{0:T(1024)S(1)}, f32[]{:T(128)}) all-reduce(f32[4096]{0:T(1024)S(1)} %exponential_multiply_fusion.5, f32[]{:T(128)} %reduce_sum.73), channel_id=1, replica_groups=mesh['item'=8,'code'=4] {'code'}, use_global_device_ids=true, to_apply=%region_10.11 | all-reduce | flops 4097 | bytes 32776 | tf_op jit(solution)/shard_map/psum | solution.py:82
  340.7 8.2 %add_reduce_fusion.4 = f32[8,8,8,64]{3,2,1,0:T(8,128)S(1)} fusion(f32[8,8,8,64,64]{3,4,2,1,0:T(8,128)} %get-tuple-element.107, f32[8,8,64]{2,1,0:T(8,128)S(1)} %add.166), kind=kLoop, calls=%fused_computation.38 | loop fusion | flops 4161536 | bytes 8536064 | tf_op jit(solution)/shard_map/reduce_max | solution.py:88
  348.9 11.1 %exponential_reduce_fusion.4 = f32[8,8,8,64]{3,2,1,0:T(8,128)S(1)} fusion(f32[8,8,8,64,64]{3,4,2,1,0:T(8,128)} %get-tuple-element.107, f32[8,8,8,64]{3,2,1,0:T(8,128)S(1)} %add_reduce_fusion.4, f32[8,8,64]{2,1,0:T(8,128)S(1)} %add.166), kind=kLoop, calls=%fused_computation.32 | loop fusion | flops 6258688 | bytes 8667136 | tf_op jit(solution)/shard_map/reduce_sum | solution.py:89
  368.5 35.2 %pmax.43 = f32[8192]{0:T(1024)S(1)} all-reduce(f32[8192]{0:T(1024)S(1)} %reshape.249), channel_id=1, replica_groups=mesh['item'=8,'code'=4] {'item'}, use_global_device_ids=true, to_apply=%region_15.16 | all-reduce | flops 8192 | bytes 65536 | tf_op jit(solution)/shard_map/pmax | solution.py:119
  403.7 33.0 %psum.59 = f32[8192]{0:T(1024)S(1)} all-reduce(f32[8192]{0:T(1024)S(1)} %exponential_multiply_fusion.2), channel_id=1, replica_groups=mesh['item'=8,'code'=4] {'item'}, use_global_device_ids=true, to_apply=%region_17.18 | all-reduce | flops 8192 | bytes 65536 | tf_op jit(solution)/shard_map/psum | solution.py:120
  446.2 7.6 %exponential_reduce_fusion.3 = f32[8,8,64]{2,1,0:T(8,128)S(1)} fusion(f32[8,8,8,64,64]{3,4,2,1,0:T(8,128)} %get-tuple-element.107, f32[8,8,64]{2,1,0:T(8,128)S(1)} %add_reduce_fusion.3, f32[8,8,8,64]{3,2,1,0:T(8,128)S(1)} %bitcast.102), kind=kLoop, calls=%fused_computation.31 | loop fusion | flops 6287360 | bytes 8552448 | tf_op jit(solution)/shard_map/reduce_sum | solution.py:75
  454.0 10.1 %pmax.44 = f32[4096]{0:T(1024)S(1)} all-reduce(f32[4096]{0:T(1024)S(1)} %reshape.254), channel_id=1, replica_groups=mesh['item'=8,'code'=4] {'code'}, use_global_device_ids=true, to_apply=%region_19.20 | all-reduce | flops 4096 | bytes 32768 | tf_op jit(solution)/shard_map/pmax | solution.py:81
  464.1 10.1 %psum.60 = f32[4096]{0:T(1024)S(1)} all-reduce(f32[4096]{0:T(1024)S(1)} %exponential_multiply_fusion.4), channel_id=1, replica_groups=mesh['item'=8,'code'=4] {'code'}, use_global_device_ids=true, to_apply=%region_21.22 | all-reduce | flops 4096 | bytes 32768 | tf_op jit(solution)/shard_map/psum | solution.py:82
  474.3 8.2 %add_reduce_fusion.2 = f32[8,8,8,64]{3,2,1,0:T(8,128)S(1)} fusion(f32[8,8,8,64,64]{3,4,2,1,0:T(8,128)} %get-tuple-element.107, f32[8,8,64]{2,1,0:T(8,128)S(1)} %add.175), kind=kLoop, calls=%fused_computation.36 | loop fusion | flops 4161536 | bytes 8536064 | tf_op jit(solution)/shard_map/reduce_max | solution.py:88
  482.5 11.1 %exponential_reduce_fusion.2 = f32[8,8,8,64]{3,2,1,0:T(8,128)S(1)} fusion(f32[8,8,8,64,64]{3,4,2,1,0:T(8,128)} %get-tuple-element.107, f32[8,8,8,64]{3,2,1,0:T(8,128)S(1)} %add_reduce_fusion.2, f32[8,8,64]{2,1,0:T(8,128)S(1)} %add.175), kind=kLoop, calls=%fused_computation.30 | loop fusion | flops 6258688 | bytes 8667136 | tf_op jit(solution)/shard_map/reduce_sum | solution.py:89
  502.1 33.0 %pmax.45 = f32[8192]{0:T(1024)S(1)} all-reduce(f32[8192]{0:T(1024)S(1)} %reshape.256), channel_id=1, replica_groups=mesh['item'=8,'code'=4] {'item'}, use_global_device_ids=true, to_apply=%region_26.27 | all-reduce | flops 8192 | bytes 65536 | tf_op jit(solution)/shard_map/pmax | solution.py:119
  535.2 33.2 %psum.61 = f32[8192]{0:T(1024)S(1)} all-reduce(f32[8192]{0:T(1024)S(1)} %exponential_multiply_fusion.1), channel_id=1, replica_groups=mesh['item'=8,'code'=4] {'item'}, use_global_device_ids=true, to_apply=%region_28.29 | all-reduce | flops 8192 | bytes 65536 | tf_op jit(solution)/shard_map/psum | solution.py:120
  584.9 10.1 %pmax.46 = f32[4096]{0:T(1024)S(1)} all-reduce(f32[4096]{0:T(1024)S(1)} %reshape.261), channel_id=1, replica_groups=mesh['item'=8,'code'=4] {'code'}, use_global_device_ids=true, to_apply=%region_30.31 | all-reduce | flops 4096 | bytes 32768 | tf_op jit(solution)/shard_map/pmax | solution.py:81
  595.0 10.1 %psum.62 = f32[4096]{0:T(1024)S(1)} all-reduce(f32[4096]{0:T(1024)S(1)} %exponential_multiply_fusion.3), channel_id=1, replica_groups=mesh['item'=8,'code'=4] {'code'}, use_global_device_ids=true, to_apply=%region_32.33 | all-reduce | flops 4096 | bytes 32768 | tf_op jit(solution)/shard_map/psum | solution.py:82
  605.2 8.2 %add_reduce_fusion = f32[8,8,8,64]{3,2,1,0:T(8,128)S(1)} fusion(f32[8,8,8,64,64]{3,4,2,1,0:T(8,128)} %get-tuple-element.107, f32[8,8,64]{2,1,0:T(8,128)S(1)} %add.183), kind=kLoop, calls=%fused_computation.34 | loop fusion | flops 4161536 | bytes 8536064 | tf_op jit(solution)/shard_map/reduce_max | solution.py:88
  613.5 11.1 %exponential_reduce_fusion = f32[8,8,8,64]{3,2,1,0:T(8,128)S(1)} fusion(f32[8,8,8,64,64]{3,4,2,1,0:T(8,128)} %get-tuple-element.107, f32[8,8,8,64]{3,2,1,0:T(8,128)S(1)} %add_reduce_fusion, f32[8,8,64]{2,1,0:T(8,128)S(1)} %add.183), kind=kLoop, calls=%fused_computation.28 | loop fusion | flops 6258688 | bytes 8667136 | tf_op jit(solution)/shard_map/reduce_sum | solution.py:89
  633.1 33.0 %pmax.47 = f32[8192]{0:T(1024)S(1)} all-reduce(f32[8192]{0:T(1024)S(1)} %reshape.263), channel_id=1, replica_groups=mesh['item'=8,'code'=4] {'item'}, use_global_device_ids=true, to_apply=%region_37.38 | all-reduce | flops 8192 | bytes 65536 | tf_op jit(solution)/shard_map/pmax | solution.py:119
  666.1 33.0 %psum.63 = f32[8192]{0:T(1024)S(1)} all-reduce(f32[8192]{0:T(1024)S(1)} %exponential_multiply_fusion), channel_id=1, replica_groups=mesh['item'=8,'code'=4] {'item'}, use_global_device_ids=true, to_apply=%region_39.40 | all-reduce | flops 8192 | bytes 65536 | tf_op jit(solution)/shard_map/psum | solution.py:120
  (206 shorter events, 214.2 us)
Async XLA Ops:
  7.2 28.2 %copy-start = (s32[64,16]{0,1:T(8,128)S(1)}, s32[64,16]{0,1:T(8,128)}, u32[]{:S(2)}) copy-start(s32[64,16]{0,1:T(8,128)} %param.17) | copy-start | bytes 12292
  7.2 39.6 %all-gather.5.cloned.1.call-start = ((), (), s32[]{:S(2)}) async-start(), calls=%async_computation.1 | async-start | bytes 5242880 | tf_op jit(solution)/shard_map/all_gather | solution.py:14
  7.9 165.5 %all-gather.3.cloned.1.call-start = ((), (), s32[]{:S(2)}) async-start(), calls=%async_computation | async-start | bytes 9437184 | tf_op jit(solution)/shard_map/all_gather | solution.py:15
  35.4 4.6 copy-start.2
  302.9 10.7 %copy-start.1 = (f32[8,8,8,64,64]{3,4,2,1,0:T(8,128)S(1)}, f32[8,8,8,64,64]{3,4,2,1,0:T(8,128)}, u32[]{:S(2)}) copy-start(f32[8,8,8,64,64]{3,4,2,1,0:T(8,128)} %get-tuple-element.107) | copy-start | bytes 25165828
  302.9 37.6 %copy-start.3 = (f32[4096]{0:T(1024)S(1)}, f32[4096]{0:T(1024)}, u32[]{:S(2)}) copy-start(f32[4096]{0:T(1024)} %param.15) | copy-start | bytes 49156
  605.2 19.4 %copy-start.4 = (f32[4096]{0:T(1024)}, f32[4096]{0:T(1024)S(1)}, u32[]{:S(2)}) copy-start(f32[4096]{0:T(1024)S(1)} %add_subtract_fusion.3) | copy-start | bytes 49156
Sparse Core Ops, SparseCore 0:
  9.5 37.1 all-gather.4
  48.9 124.4 all-gather.2
where the time goes:
time: 708 us; the launch traced here: 707 us
  blocking collectives  286 us (40%)
  waiting for transfers between devices  127 us (18%)
  other arithmetic  127 us (18%)
  local copies, waits for them, and re-layouts  85.9 us (12%)
  matrix products  59.6 us (8%)
  between operations  15.8 us (2%)
    all_gather x1, waiting for transfers between devices, body(): code_cols = lax.all_gather(codebook, 'item', axis=0, tiled=True)  121 us
    pmax x3, blocking collectives, body(): joined_peak = lax.pmax(col_peak, 'item')  101 us
    psum x3, blocking collectives, body(): joined_total = lax.psum(col_total * jnp.exp(col_peak - joined_peak), 'item')  99.3 us
    dot_general x8, matrix products, build_tiles(): jnp.einsum('rbi,rbsj->bsij', own, picked, precision=lax.Precision.HIGHEST)  58.1 us
    gather x8, local copies, waits for them, and re-layouts, build_tiles(): picked = code_column_splits[:, ids, :]  49.4 us
    reduce_sum x3, other arithmetic, col_reduce(): block_total = jnp.sum(jnp.exp(logits - block_peak[:, :, None, :]), axis=2)  33.2 us
    psum x3, blocking collectives, body(): merged_total = lax.psum(row_total * jnp.exp(row_peak - merged_peak), 'code')  31.6 us
    pmax x3, blocking collectives, body(): merged_peak = lax.pmax(row_peak, 'code')  30.4 us
  transfers between devices with their start and end apart: 2, of which 2 were waited for; matrix products, arithmetic and copies ran while one was open for 2% of the time, Pallas kernels for 0%

commit v1 on v0

--- a/solution.py
+++ b/solution.py
@@ -12,7 +12,12 @@
 
 def body(residuals, codebook, item_weight, code_capacity, pairs):
     item_columns = lax.all_gather(residuals, "code", axis=0, tiled=True)
-    code_cols = lax.all_gather(codebook, "item", axis=0, tiled=True)
+    ring = [codebook]
+    for hop in range(7):
+        ring.append(lax.ppermute(ring[-1], "item", [(dev, (dev + 1) % 8) for dev in range(8)]))
+    code_cols = jnp.roll(
+        jnp.concatenate(ring[::-1], axis=0), (lax.axis_index("item") + 1) * ring[0].shape[0], axis=0
+    )
     embedding_width = item_columns.shape[0]
     item_count = item_columns.shape[1]
     code_count = code_cols.shape[1]

time: 708 us -> 814 us (1.15)
  local copies, waits for them, and re-layouts: 85.9 us -> 160 us
  waiting for transfers between devices: 127 us -> 147 us
  blocking collectives: 286 us -> 295 us
    ppermute x0 -> x7, waiting for transfers between devices: none -> 147 us  [body(): lax.ppermute(ring[-1], 'item', [(dev, (dev + 1) % 8) for dev in range(8)])]
    all_gather x1 -> x0, waiting for transfers between devices: 121 us -> none  [body(): code_cols = lax.all_gather(codebook, 'item', axis=0, tiled=True)]
    concatenate x0 -> x1, local copies, waits for them, and re-layouts: none -> 46.3 us  [body(): jnp.roll(jnp.concatenate(ring[::-1], axis=0), (lax.axis_index('item') + 1...]
    ppermute x0 -> x7, local copies, waits for them, and re-layouts: none -> 23.3 us  [body(): lax.ppermute(ring[-1], 'item', [(dev, (dev + 1) % 8) for dev in range(8)])]
    dynamic_slice x0 -> x1, local copies, waits for them, and re-layouts: none -> 10 us  [body(): jnp.roll(jnp.concatenate(ring[::-1], axis=0), (lax.axis_index('item') + 1...]
    psum x1, blocking collectives: 23.8 us -> 33 us  [body(): weight_sum = lax.psum(jnp.sum(item_weight), 'item')]
    all_gather x1 -> x0, local copies, waits for them, and re-layouts: 9 us -> none  [body(): code_cols = lax.all_gather(codebook, 'item', axis=0, tiled=True)]
  transfers between devices with their start and end apart: 2 -> 8, of which waited for: 2 -> 6; matrix products, arithmetic and copies ran while one was open for 2% -> 5% of each run, Pallas kernels for 0% -> 0%
where the time goes in v1:
time: 814 us; the launch traced here: 811 us
  blocking collectives  295 us (36%)
  local copies, waits for them, and re-layouts  160 us (20%)
  waiting for transfers between devices  147 us (18%)
  other arithmetic  126 us (15%)
  matrix products  59.6 us (7%)
  between operations  15.9 us (2%)
    ppermute x7, waiting for transfers between devices, body(): lax.ppermute(ring[-1], 'item', [(dev, (dev + 1) % 8) for dev in range(8)])  147 us
    pmax x3, blocking collectives, body(): joined_peak = lax.pmax(col_peak, 'item')  101 us
    psum x3, blocking collectives, body(): joined_total = lax.psum(col_total * jnp.exp(col_peak - joined_peak), 'item')  99.3 us
    dot_general x8, matrix products, build_tiles(): jnp.einsum('rbi,rbsj->bsij', own, picked, precision=lax.Precision.HIGHEST)  58.1 us
    gather x8, local copies, waits for them, and re-layouts, build_tiles(): picked = code_column_splits[:, ids, :]  49 us
    concatenate x1, local copies, waits for them, and re-layouts, body(): jnp.roll(jnp.concatenate(ring[::-1], axis=0), (lax.axis_index('item') + 1...  46.3 us
    reduce_sum x3, other arithmetic, col_reduce(): block_total = jnp.sum(jnp.exp(logits - block_peak[:, :, None, :]), axis=2)  33.2 us
    psum x1, blocking collectives, body(): weight_sum = lax.psum(jnp.sum(item_weight), 'item')  33 us
  transfers between devices with their start and end apart: 8, of which 6 were waited for; matrix products, arithmetic and copies ran while one was open for 5% of the time, Pallas kernels for 0%

profile of v1, /device:TPU:0, one launch (start us, length us, event | category | flops | bytes accessed | tf_op | source)
XLA Modules:
  0.0 811.5 jit_solution(7034454668111535694)
XLA Ops:
  10.3 26.4 %collective-permute-done = f32[32,8192]{1,0:T(8,128)S(1)} collective-permute-done((f32[32,8192]{1,0:T(8,128)}, f32[32,8192]{1,0:T(8,128)S(1)}, u32[]{:S(2)}, u32[]{:S(2)}) %collective-permute-start) | collective-permute-done | bytes 1048608 | tf_op jit(solution)/shard_map/ppermute | solution.py:17
  36.7 27.0 %collective-permute-done.1 = f32[32,8192]{1,0:T(8,128)S(1)} collective-permute-done((f32[32,8192]{1,0:T(8,128)S(1)}, f32[32,8192]{1,0:T(8,128)S(1)}, u32[]{:S(2)}, u32[]{:S(2)}) %collective-permute-start.1) | collective-permute-done | bytes 1048608 | tf_op jit(solution)/shard_map/ppermute | solution.py:17
  63.7 26.2 %collective-permute-done.2 = f32[32,8192]{1,0:T(8,128)S(1)} collective-permute-done((f32[32,8192]{1,0:T(8,128)S(1)}, f32[32,8192]{1,0:T(8,128)S(1)}, u32[]{:S(2)}, u32[]{:S(2)}) %collective-permute-start.2) | collective-permute-done | bytes 1048608 | tf_op jit(solution)/shard_map/ppermute | solution.py:17
  89.9 25.3 %collective-permute-done.3 = f32[32,8192]{1,0:T(8,128)S(1)} collective-permute-done((f32[32,8192]{1,0:T(8,128)S(1)}, f32[32,8192]{1,0:T(8,128)S(1)}, u32[]{:S(2)}, u32[]{:S(2)}) %collective-permute-start.3) | collective-permute-done | bytes 1048608 | tf_op jit(solution)/shard_map/ppermute | solution.py:17
  116.2 24.6 %collective-permute-done.4 = f32[32,8192]{1,0:T(8,128)} collective-permute-done((f32[32,8192]{1,0:T(8,128)S(1)}, f32[32,8192]{1,0:T(8,128)}, u32[]{:S(2)}, u32[]{:S(2)}) %collective-permute-start.4) | collective-permute-done | bytes 1048608 | tf_op jit(solution)/shard_map/ppermute | solution.py:17
  147.6 17.2 %collective-permute-done.5 = f32[32,8192]{1,0:T(8,128)} collective-permute-done((f32[32,8192]{1,0:T(8,128)}, f32[32,8192]{1,0:T(8,128)}, u32[]{:S(2)}, u32[]{:S(2)}) %collective-permute-start.5) | collective-permute-done | bytes 1048608 | tf_op jit(solution)/shard_map/ppermute | solution.py:17
  164.7 33.0 %psum.56 = f32[]{:T(128)} all-reduce(f32[]{:T(128)} %reduce_sum.72), channel_id=1, replica_groups=mesh['item'=8,'code'=4] {'item'}, use_global_device_ids=true, to_apply=%region_1.2 | all-reduce | flops 1 | bytes 8 | tf_op jit(solution)/shard_map/psum | solution.py:27
  232.0 46.3 %concatenate.15 = f32[512,8192]{0,1:T(8,128)} concatenate(f32[32,8192]{0,1:T(8,128)} %copy.54, f32[32,8192]{0,1:T(8,128)} %copy.55, f32[32,8192]{0,1:T(8,128)} %copy.56, f32[32,8192]{0,1:T(8,128)} %copy.57, f32[32,8192]{0,1:T(8,128)} %copy.58, f32[32,8192]{0,1:T(8,128)} %copy.59, f32[32,8192]{0,1:T(8,128)} %copy.60, f32[32,8192]{0,1:T(8,128)} %copy.61, f32[32,8192]{0,1:T(8,128)} %copy.54, ...), dimensions={0} | concatenate | bytes 33554432 | tf_op jit(solution)/shard_map/jit(_roll_dynamic)/concatenate | solution.py:18
  288.3 119.5 %while.43 = (s32[]{:T(128)}, f32[8,8,8,64,64]{3,4,2,1,0:T(8,128)}, s32[8]{0:T(128)S(1)}, pred[64,8]{0,1:T(8,128)(4,1)S(1)}, s32[64,8]{0,1:T(8,128)S(1)}, /*index...) while((s32[]{:T(128)}, f32[8,8,8,64,64]{3,4,2,1,0:T(8,128)}, ...), condition=%wide.region_4.5_spmd, body=%wide.region_3.4_spmd.sunk | while | flops 805831872 | bytes 15212019 | solution.py:60
  423.9 10.2 %pmax.42 = f32[4096]{0:T(1024)S(1)} all-reduce(f32[4096]{0:T(1024)S(1)} %reshape.247), channel_id=1, replica_groups=mesh['item'=8,'code'=4] {'code'}, use_global_device_ids=true, to_apply=%region_8.9 | all-reduce | flops 4096 | bytes 32768 | tf_op jit(solution)/shard_map/pmax | solution.py:86
  434.1 11.4 %all-reduce.3 = (f32[4096]{0:T(1024)S(1)}, f32[]{:T(128)}) all-reduce(f32[4096]{0:T(1024)S(1)} %exponential_multiply_fusion.5, f32[]{:T(128)} %reduce_sum.73), channel_id=1, replica_groups=mesh['item'=8,'code'=4] {'code'}, use_global_device_ids=true, to_apply=%region_10.11 | all-reduce | flops 4097 | bytes 32776 | tf_op jit(solution)/shard_map/psum | solution.py:87
  453.8 11.1 %exponential_reduce_fusion.4 = f32[8,8,8,64]{3,2,1,0:T(8,128)S(1)} fusion(f32[8,8,8,64,64]{3,4,2,1,0:T(8,128)} %get-tuple-element.107, f32[8,8,8,64]{3,2,1,0:T(8,128)S(1)} %add_reduce_fusion.4, f32[8,8,64]{2,1,0:T(8,128)S(1)} %add.182), kind=kLoop, calls=%fused_computation.32 | loop fusion | flops 6258688 | bytes 8667136 | tf_op jit(solution)/shard_map/reduce_sum | solution.py:94
  473.4 35.1 %pmax.43 = f32[8192]{0:T(1024)S(1)} all-reduce(f32[8192]{0:T(1024)S(1)} %reshape.249), channel_id=1, replica_groups=mesh['item'=8,'code'=4] {'item'}, use_global_device_ids=true, to_apply=%region_15.16 | all-reduce | flops 8192 | bytes 65536 | tf_op jit(solution)/shard_map/pmax | solution.py:124
  508.6 33.0 %psum.59 = f32[8192]{0:T(1024)S(1)} all-reduce(f32[8192]{0:T(1024)S(1)} %exponential_multiply_fusion.2), channel_id=1, replica_groups=mesh['item'=8,'code'=4] {'item'}, use_global_device_ids=true, to_apply=%region_17.18 | all-reduce | flops 8192 | bytes 65536 | tf_op jit(solution)/shard_map/psum | solution.py:125
  558.8 10.1 %pmax.44 = f32[4096]{0:T(1024)S(1)} all-reduce(f32[4096]{0:T(1024)S(1)} %reshape.254), channel_id=1, replica_groups=mesh['item'=8,'code'=4] {'code'}, use_global_device_ids=true, to_apply=%region_19.20 | all-reduce | flops 4096 | bytes 32768 | tf_op jit(solution)/shard_map/pmax | solution.py:86
  568.9 10.1 %psum.60 = f32[4096]{0:T(1024)S(1)} all-reduce(f32[4096]{0:T(1024)S(1)} %exponential_multiply_fusion.4), channel_id=1, replica_groups=mesh['item'=8,'code'=4] {'code'}, use_global_device_ids=true, to_apply=%region_21.22 | all-reduce | flops 4096 | bytes 32768 | tf_op jit(solution)/shard_map/psum | solution.py:87
  587.4 11.1 %exponential_reduce_fusion.2 = f32[8,8,8,64]{3,2,1,0:T(8,128)S(1)} fusion(f32[8,8,8,64,64]{3,4,2,1,0:T(8,128)} %get-tuple-element.107, f32[8,8,8,64]{3,2,1,0:T(8,128)S(1)} %add_reduce_fusion.2, f32[8,8,64]{2,1,0:T(8,128)S(1)} %add.191), kind=kLoop, calls=%fused_computation.30 | loop fusion | flops 6258688 | bytes 8667136 | tf_op jit(solution)/shard_map/reduce_sum | solution.py:94
  607.0 33.0 %pmax.45 = f32[8192]{0:T(1024)S(1)} all-reduce(f32[8192]{0:T(1024)S(1)} %reshape.256), channel_id=1, replica_groups=mesh['item'=8,'code'=4] {'item'}, use_global_device_ids=true, to_apply=%region_26.27 | all-reduce | flops 8192 | bytes 65536 | tf_op jit(solution)/shard_map/pmax | solution.py:124
  640.0 33.2 %psum.61 = f32[8192]{0:T(1024)S(1)} all-reduce(f32[8192]{0:T(1024)S(1)} %exponential_multiply_fusion.1), channel_id=1, replica_groups=mesh['item'=8,'code'=4] {'item'}, use_global_device_ids=true, to_apply=%region_28.29 | all-reduce | flops 8192 | bytes 65536 | tf_op jit(solution)/shard_map/psum | solution.py:125
  689.8 10.1 %pmax.46 = f32[4096]{0:T(1024)S(1)} all-reduce(f32[4096]{0:T(1024)S(1)} %reshape.261), channel_id=1, replica_groups=mesh['item'=8,'code'=4] {'code'}, use_global_device_ids=true, to_apply=%region_30.31 | all-reduce | flops 4096 | bytes 32768 | tf_op jit(solution)/shard_map/pmax | solution.py:86
  699.9 10.1 %psum.62 = f32[4096]{0:T(1024)S(1)} all-reduce(f32[4096]{0:T(1024)S(1)} %exponential_multiply_fusion.3), channel_id=1, replica_groups=mesh['item'=8,'code'=4] {'code'}, use_global_device_ids=true, to_apply=%region_32.33 | all-reduce | flops 4096 | bytes 32768 | tf_op jit(solution)/shard_map/psum | solution.py:87
  718.3 11.1 %exponential_reduce_fusion = f32[8,8,8,64]{3,2,1,0:T(8,128)S(1)} fusion(f32[8,8,8,64,64]{3,4,2,1,0:T(8,128)} %get-tuple-element.107, f32[8,8,8,64]{3,2,1,0:T(8,128)S(1)} %add_reduce_fusion, f32[8,8,64]{2,1,0:T(8,128)S(1)} %add.199), kind=kLoop, calls=%fused_computation.28 | loop fusion | flops 6258688 | bytes 8667136 | tf_op jit(solution)/shard_map/reduce_sum | solution.py:94
  737.9 33.0 %pmax.47 = f32[8192]{0:T(1024)S(1)} all-reduce(f32[8192]{0:T(1024)S(1)} %reshape.263), channel_id=1, replica_groups=mesh['item'=8,'code'=4] {'item'}, use_global_device_ids=true, to_apply=%region_37.38 | all-reduce | flops 8192 | bytes 65536 | tf_op jit(solution)/shard_map/pmax | solution.py:124
  771.0 33.0 %psum.63 = f32[8192]{0:T(1024)S(1)} all-reduce(f32[8192]{0:T(1024)S(1)} %exponential_multiply_fusion), channel_id=1, replica_groups=mesh['item'=8,'code'=4] {'item'}, use_global_device_ids=true, to_apply=%region_39.40 | all-reduce | flops 8192 | bytes 65536 | tf_op jit(solution)/shard_map/psum | solution.py:125
  (236 shorter events, 289.2 us)
Async XLA Ops:
  7.2 135.2 %copy-start = (s32[64,16]{0,1:T(8,128)S(1)}, s32[64,16]{0,1:T(8,128)}, u32[]{:S(2)}) copy-start(s32[64,16]{0,1:T(8,128)} %param.17) | copy-start | bytes 12292
  7.2 215.7 %all-gather.2.cloned.1.call-start = ((), (), s32[]{:S(2)}) async-start(), calls=%async_computation | async-start | bytes 5242880 | tf_op jit(solution)/shard_map/all_gather | solution.py:14
  7.2 29.5 %collective-permute-start = (f32[32,8192]{1,0:T(8,128)}, f32[32,8192]{1,0:T(8,128)S(1)}, u32[]{:S(2)}, u32[]{:S(2)}) collective-permute-start(f32[32,8192]{1,0:T(8,128)} %param.14), channel_id=1, source_target_pairs={{0,4},{4,8},{8,12},{12,16},{16,20},{20,24},{24,28},{28,0},{1,5},{5... | collective-permute-start | bytes 3145736 | tf_op jit(solution)/shard_map/ppermute | solution.py:17
  36.7 27.0 %collective-permute-start.1 = (f32[32,8192]{1,0:T(8,128)S(1)}, f32[32,8192]{1,0:T(8,128)S(1)}, u32[]{:S(2)}, u32[]{:S(2)}) collective-permute-start(f32[32,8192]{1,0:T(8,128)S(1)} %collective-permute-done), channel_id=1, source_target_pairs={{0,4},{4,8},{8,12},{12,16},{16,20},{20,24},{24,28},{28,0},{1,5},{5... | collective-permute-start | bytes 3145736 | tf_op jit(solution)/shard_map/ppermute | solution.py:17
  63.7 26.2 %collective-permute-start.2 = (f32[32,8192]{1,0:T(8,128)S(1)}, f32[32,8192]{1,0:T(8,128)S(1)}, u32[]{:S(2)}, u32[]{:S(2)}) collective-permute-start(f32[32,8192]{1,0:T(8,128)S(1)} %collective-permute-done.1), channel_id=1, source_target_pairs={{0,4},{4,8},{8,12},{12,16},{16,20},{20,24},{24,28},{28,0},{1,5},{5... | collective-permute-start | bytes 3145736 | tf_op jit(solution)/shard_map/ppermute | solution.py:17
  89.9 52.3 %copy-start.3 = (f32[32,8192]{1,0:T(8,128)}, f32[32,8192]{1,0:T(8,128)S(1)}, u32[]{:S(2)}) copy-start(f32[32,8192]{1,0:T(8,128)S(1)} %collective-permute-done.2) | copy-start | bytes 3145732
  89.9 25.3 %collective-permute-start.3 = (f32[32,8192]{1,0:T(8,128)S(1)}, f32[32,8192]{1,0:T(8,128)S(1)}, u32[]{:S(2)}, u32[]{:S(2)}) collective-permute-start(f32[32,8192]{1,0:T(8,128)S(1)} %collective-permute-done.2), channel_id=1, source_target_pairs={{0,4},{4,8},{8,12},{12,16},{16,20},{20,24},{24,28},{28,0},{1,5},{5... | collective-permute-start | bytes 3145736 | tf_op jit(solution)/shard_map/ppermute | solution.py:17
  115.2 1.0 copy-start.4
  116.2 24.6 %collective-permute-start.4 = (f32[32,8192]{1,0:T(8,128)S(1)}, f32[32,8192]{1,0:T(8,128)}, u32[]{:S(2)}, u32[]{:S(2)}) collective-permute-start(f32[32,8192]{1,0:T(8,128)S(1)} %collective-permute-done.3), channel_id=1, source_target_pairs={{0,4},{4,8},{8,12},{12,16},{16,20},{20,24},{24,28},{28,0},{1,5},{5... | collective-permute-start | bytes 3145736 | tf_op jit(solution)/shard_map/ppermute | solution.py:17
  140.8 24.0 %collective-permute-start.5 = (f32[32,8192]{1,0:T(8,128)}, f32[32,8192]{1,0:T(8,128)}, u32[]{:S(2)}, u32[]{:S(2)}) collective-permute-start(f32[32,8192]{1,0:T(8,128)} %collective-permute-done.4), channel_id=1, source_target_pairs={{0,4},{4,8},{8,12},{12,16},{16,20},{20,24},{24,28},{28,0},{1,5},{5... | collective-permute-start | bytes 3145736 | tf_op jit(solution)/shard_map/ppermute | solution.py:17
  142.4 4.6 copy-start.7
  142.4 55.3 %copy-start.2 = (f32[32,8192]{1,0:T(8,128)S(1)}, f32[32,8192]{1,0:T(8,128)}, u32[]{:S(2)}) copy-start(f32[32,8192]{1,0:T(8,128)} %param.14) | copy-start | bytes 3145732
  142.4 58.2 %copy-start.5 = (f32[8192]{0:T(1024)S(1)}, f32[8192]{0:T(1024)}, u32[]{:S(2)}) copy-start(f32[8192]{0:T(1024)} %param.16) | copy-start | bytes 98308
  164.7 63.7 %collective-permute-start.6 = (f32[32,8192]{1,0:T(8,128)}, f32[32,8192]{1,0:T(8,128)}, u32[]{:S(2)}, u32[]{:S(2)}) collective-permute-start(f32[32,8192]{1,0:T(8,128)} %collective-permute-done.5), channel_id=1, source_target_pairs={{0,4},{4,8},{8,12},{12,16},{16,20},{20,24},{24,28},{28,0},{1,5},{5... | collective-permute-start | bytes 3145736 | tf_op jit(solution)/shard_map/ppermute | solution.py:17
  407.9 10.7 %copy-start.1 = (f32[8,8,8,64,64]{3,4,2,1,0:T(8,128)S(1)}, f32[8,8,8,64,64]{3,4,2,1,0:T(8,128)}, u32[]{:S(2)}) copy-start(f32[8,8,8,64,64]{3,4,2,1,0:T(8,128)} %get-tuple-element.107) | copy-start | bytes 25165828
  407.9 37.6 %copy-start.8 = (f32[4096]{0:T(1024)S(1)}, f32[4096]{0:T(1024)}, u32[]{:S(2)}) copy-start(f32[4096]{0:T(1024)} %param.15) | copy-start | bytes 49156
  453.8 88.5 %copy-start.6 = (f32[8192]{0:T(1024)S(1)}, f32[8192]{0:T(1024)}, u32[]{:S(2)}) copy-start(f32[8192]{0:T(1024)} %param.16) | copy-start | bytes 98308
  710.0 19.4 %copy-start.9 = (f32[4096]{0:T(1024)}, f32[4096]{0:T(1024)S(1)}, u32[]{:S(2)}) copy-start(f32[4096]{0:T(1024)S(1)} %add_subtract_fusion.3) | copy-start | bytes 49156
Sparse Core Ops, SparseCore 0:
  36.8 35.8 all-gather.1
